TPU v7x, 32 devices: a whole 2x2x4 slice. The times are simulated.
32 devices in a mesh: group: 2 (over x), wide: 16 (over z, y, core).
Axes of the slice: x: 2, y: 2, z: 4, core: 2. Of those that a mesh axis runs over, the one named last changes fastest.
Arguments:
- stream_index: int32 [2], P('group'), parts along dimension 0, may hold values from 0 to 16777215
- forcing: bfloat16 [32, 1536, 1536], P('group', 'wide'), parts along dimension 0, may hold values from -144 to 144
Outputs:
- pressure: bfloat16 [32, 1536, 1536], P('group', 'wide'), parts along dimension 0
There are 2 independent parts, one for each index of `group`. A program takes and returns all parts, laid end to end along the dimension named above; each array names one. Nothing has to cross between parts.
All inputs are finite; a program needn't handle non-finite values.
Results may differ from a plain program's by a relative error of at most 0.0045.
Values may be sent and summed in bfloat16 or wider, within the bound.
No kernel may reach another device: no remote copies, remote signals or barrier semaphores. Data moves between devices by JAX's collectives and lax.ppermute only.
A program may use at most 192 MiB of HBM per device.

v0:
```python
import math
import jax
import jax.numpy as jnp
from jax import lax
from jax.sharding import PartitionSpec as P

LEN_X = 1536
LEN_Y = 1536
ITERS = 4


def with_halo(block, sides, width):
    for axis, dim in sides:
        count = lax.axis_size(axis)
        forward = [(i, i + 1) for i in range(count - 1)]
        backward = [(target, source) for source, target in forward]
        low = lax.ppermute(
            lax.slice_in_dim(block, block.shape[dim] - width, None, axis=dim), axis, forward
        )
        high = lax.ppermute(lax.slice_in_dim(block, 0, width, axis=dim), axis, backward)
        block = jnp.concatenate([low, block, high], axis=dim)
    return block


def scramble(value):
    value = value ^ value >> 16 & 65535
    value = value * 73244475
    value = value ^ value >> 16 & 65535
    value = value * 73244475
    value = value ^ value >> 16 & 65535
    return value


def cosine_basis(length):
    row_idx = lax.broadcasted_iota(jnp.int32, (length, length), 0)
    mode_idx = lax.broadcasted_iota(jnp.int32, (length, length), 1)
    phase = (2 * row_idx + 1) * mode_idx % (4 * length)
    angle = phase.astype(jnp.float32) * (math.pi / (2.0 * length))
    weights = jnp.where(mode_idx == 0, math.sqrt(1.0 / length), math.sqrt(2.0 / length))
    return (weights * jnp.cos(angle)).astype(jnp.bfloat16)


def coefficient_plane(stream_key, mode_z, depth):
    mode_x = lax.broadcasted_iota(jnp.int32, (LEN_X, LEN_Y), 0)
    mode_y = lax.broadcasted_iota(jnp.int32, (LEN_X, LEN_Y), 1)
    counter = (mode_z * LEN_X + mode_x) * LEN_Y + mode_y
    bits_a = scramble(2 * counter ^ stream_key)
    bits_b = scramble(2 * counter + 1 ^ stream_key)
    uniform_a = (bits_a >> 8 & 16777215).astype(jnp.float32) * 2.0 ** (-24) + 2.0 ** (-25)
    uniform_b = (bits_b >> 8 & 16777215).astype(jnp.float32) * 2.0 ** (-24) + 2.0 ** (-25)
    noise = jnp.sqrt(-2.0 * jnp.log(uniform_a)) * jnp.cos(2.0 * math.pi * uniform_b)
    freq_x = mode_x.astype(jnp.float32) * (math.pi / LEN_X)
    freq_y = mode_y.astype(jnp.float32) * (math.pi / LEN_Y)
    freq_z = mode_z.astype(jnp.float32) * (math.pi / depth)
    amplitude = 1.0 / jnp.sqrt(0.05 + freq_x * freq_x + freq_y * freq_y + freq_z * freq_z)
    return (amplitude * noise).astype(jnp.bfloat16)


def contract_last(left, table):
    return lax.dot_general(
        left, table, (((left.ndim - 1,), (1,)), ((), ())), preferred_element_type=jnp.float32
    )


def operate(wide_p, wide_k):
    center_p = wide_p[:, 1:-1]
    center_k = wide_k[:, 1:-1]
    total = 0.5 * (center_k + wide_k[:, 2:]) * (center_p - wide_p[:, 2:])
    total = total + 0.5 * (center_k + wide_k[:, :-2]) * (center_p - wide_p[:, :-2])
    for axis in (0, 2):
        widths = [(0, 0), (0, 0), (0, 0)]
        widths[axis] = (1, 1)
        padded_p = jnp.pad(center_p, widths)
        padded_k = jnp.pad(center_k, widths)
        size_here = center_p.shape[axis]
        for start in (0, 2):
            near_p = lax.slice_in_dim(padded_p, start, start + size_here, axis=axis)
            near_k = lax.slice_in_dim(padded_k, start, start + size_here, axis=axis)
            total = total + 0.5 * (center_k + near_k) * (center_p - near_p)
    return total


def body(stream_index, forcing):
    depth = forcing.shape[0]
    planes_here = depth // lax.axis_size("wide")
    stream_key = scramble(stream_index[0] ^ 1540483477)
    basis_x = cosine_basis(LEN_X)
    basis_y = cosine_basis(LEN_Y)
    basis_z = cosine_basis(depth)
    first_mode = lax.axis_index("wide") * planes_here
    own_modes = first_mode + jnp.arange(planes_here, dtype=jnp.int32)

    def rows_for(mode_z):
        coeff = coefficient_plane(stream_key, mode_z, depth)
        return jnp.dot(basis_x, coeff, preferred_element_type=jnp.float32).astype(jnp.bfloat16)

    def both_axes(mode_z):
        return contract_last(rows_for(mode_z), basis_y).astype(jnp.bfloat16)

    planes = lax.map(both_axes, own_modes)
    block = lax.all_to_all(planes, "wide", split_axis=1, concat_axis=0, tiled=True)
    count_z, count_x, count_y = block.shape
    field = jnp.dot(
        basis_z, block.reshape(count_z, count_x * count_y), preferred_element_type=jnp.float32
    )
    field = field.reshape(count_z, count_x, count_y)
    perm = jnp.exp(1.5 * jnp.tanh(2.0 * field))
    source = forcing.astype(jnp.float32)
    theta = 27.9
    delta = 26.1
    sigma = theta / delta
    rho = 1.0 / sigma
    step = source / theta
    press = step
    perm_wide = with_halo(perm.astype(jnp.bfloat16), (("wide", 1),), 1).astype(perm.dtype)
    for count in range(ITERS - 1):
        press_wide = with_halo(press, (("wide", 1),), 1)
        resid = source - operate(press_wide, perm_wide)
        rho_next = 1.0 / (2.0 * sigma - rho)
        step = rho_next * rho * step + 2.0 * rho_next / delta * resid
        press = press + step
        rho = rho_next
    return press.astype(jnp.bfloat16)


def solution(mesh):
    return jax.shard_map(
        body,
        mesh=mesh,
        in_specs=(P("group"), P("group", "wide", None)),
        out_specs=P("group", "wide", None),
        check_vma=False,
    )
```

profile of v0, /device:TPU:18, one launch (start us, length us, event | category | flops | bytes accessed | tf_op | source)
XLA Modules:
  0.0 644.1 jit_solution(15394397886811121742)
XLA Ops:
  0.7 36.9 %fusion.145 = bf16[1536,1536]{1,0:T(8,128)(2,1)S(1)} fusion(s32[1536]{0:T(1024)S(1)} %get-tuple-element.48, f32[1536]{0:T(1024)S(1)} %get-tuple-element.50), kind=kLoop, calls=%fused_computation.60.clone.clone.1 | loop fusion | flops 25952256 | bytes 4730880 | tf_op jit(solution)/shard_map/while/body/eval_jaxpr/dot_general | solution.py:60
  37.6 45.8 %multiply_convert_fusion.5 = bf16[1536,1536]{1,0:T(8,128)(2,1)S(1)} fusion(s32[]{:T(128)S(6)} %xor.65, s32[1536]{0:T(1024)S(1)} %get-tuple-element.47, f32[]{:T(128)S(6)} %mul.293, f32[1536]{0:T(1024)S(1)} %get-tuple-element.49, f32[1536]{0:T(1024)S(1)} %broadcast_add_fusion), kind=kLoop, calls=%fused_computation.101.clone.clone.2 | loop fusion | flops 103809024 | bytes 4737032 | tf_op jit(solution)/shard_map/while/body/eval_jaxpr/dot_general | solution.py:95
  83.4 42.3 %convolution_convert_fusion.1 = bf16[1536,1536]{1,0:T(8,128)(2,1)S(1)} fusion(s32[1536]{0:T(1024)S(1)} %get-tuple-element.48, f32[1536]{0:T(1024)S(1)} %get-tuple-element.50, bf16[1536,1536]{1,0:T(8,128)(2,1)S(1)} %multiply_convert_fusion.5), kind=kOutput, calls=%fused_computation.107 | convolution fusion | flops 7276068864 | bytes 9449472 | tf_op jit(solution)/shard_map/while/body/eval_jaxpr/dot_general | solution.py:95
  125.7 8.0 %fusion.71 = bf16[1,1536,1536]{2,1,0:T(8,128)(2,1)S(1)} fusion(bf16[1536,1536]{1,0:T(8,128)(2,1)S(1)} %convolution_convert_fusion.1, bf16[1536,1536]{1,0:T(8,128)(2,1)S(1)} %fusion.145), kind=kOutput, calls=%fused_computation.108 | convolution fusion | flops 7250116608 | bytes 14155776 | tf_op jit(solution)/shard_map/while/body/eval_jaxpr/dot_general | solution.py:60
  133.7 52.2 %copy.30 = bf16[1,1536,1536]{2,0,1:T(2,128)(2,1)} copy(bf16[1,1536,1536]{2,1,0:T(8,128)(2,1)S(1)} %fusion.71) | data formatting | bytes 9437184 | tf_op jit(solution)/shard_map/while/body/jit(dynamic_update_index_in_dim)/broadcast_in_dim | solution.py:100
  186.5 31.9 %reduce.2 = bf16[1536,1536]{1,0:T(8,128)(2,1)} reduce(bf16[1536,1,1536]{2,1,0:T(2,128)(2,1)} %bitcast.21, bf16[]{:T(256)} %broadcast.337), dimensions={1}, to_apply=%bitcast.20.reduce_sub_computation | reduce | bytes 9437186
  218.4 11.8 %reshape.15 = bf16[16,2,73728]{2,1,0:T(2,128)(2,1)} reshape(bf16[1536,1536]{1,0:T(8,128)(2,1)} %reduce.2) | data formatting | bytes 9437184
  230.2 6.7 %all-to-all-start = ((bf16[16,2,73728]{2,1,0:T(2,128)(2,1)}), bf16[16,2,73728]{2,1,0:T(2,128)(2,1)}, u32[]{:S(2)}, u32[]{:S(2)}) async-start(bf16[16,2,73728]{2,1,0:T(2,128)(2,1)} %reshape.15), calls=%async_computation | async-start | bytes 9437184 | tf_op jit(solution)/shard_map/all_to_all | solution.py:101
  237.0 9.6 %convert_multiply_fusion.1 = f32[16,96,1536]{2,0,1:T(8,128)} fusion(bf16[16,96,1536]{2,1,0:T(8,128)(2,1)} %param.3), kind=kLoop, calls=%fused_computation.4 | loop fusion | flops 4718592 | bytes 14155776 | tf_op jit(solution)/shard_map/div | solution.py:113
  246.6 94.1 %all-to-all-done = bf16[16,2,73728]{2,1,0:T(2,128)(2,1)} async-done(((bf16[16,2,73728]{2,1,0:T(2,128)(2,1)}), bf16[16,2,73728]{2,1,0:T(2,128)(2,1)}, u32[]{:S(2)}, u32[]{:S(2)}) %all-to-all-start) | async-done | bytes 4718624 | tf_op jit(solution)/shard_map/all_to_all | solution.py:101
  340.7 12.8 %reshape.16 = bf16[1536,1,1536]{2,1,0:T(2,128)(2,1)} reshape(bf16[16,2,73728]{2,1,0:T(2,128)(2,1)} %all-to-all-done) | data formatting | bytes 9437184
  353.5 31.3 %bitcast_reduce_fusion = bf16[1536,1536]{1,0:T(8,128)(2,1)} fusion(bf16[1536,1,1536]{2,1,0:T(2,128)(2,1)} %reshape.16), kind=kLoop, calls=%fused_computation.181 | loop fusion | bytes 9437184 | tf_op jit(solution)/shard_map/all_to_all | solution.py:101
  384.9 5.2 reshape.12
  390.1 5.1 exponential_convert_fusion
  397.1 4.5 collective-permute-start.1
  407.9 5.0 slice.154
  414.7 59.3 %fusion = (f32[16,96,1536]{2,0,1:T(8,128)}, f32[16,96,1536]{2,0,1:T(8,128)}) fusion(bf16[16,96,1536]{2,1,0:T(8,128)(2,1)} %param.3, f32[16,96,1536]{2,0,1:T(8,128)} %slice.154, f32[16,96,1536]{2,0,1:T(8,128)} %convert_multiply_fusion.1, f32[16,1,1536]{2,0,1:T(8,128)S(1)} %collective-permute-done.3, f32[16,98,1536]{2,0,1:T(8,128)} %copy-done, ...), kind=kLoop, calls=%fused_computation.14 | loop fusion | flops 89653248 | bytes 70975488 | tf_op jit(solution)/shard_map/add | solution.py:121
  475.0 4.1 collective-permute-start.4
  481.2 4.6 collective-permute-done.5
  485.9 69.9 %fusion.92 = (f32[16,96,1536]{2,0,1:T(8,128)}, f32[16,96,1536]{2,0,1:T(8,128)}) fusion(f32[16,96,1536]{2,0,1:T(8,128)} %get-tuple-element.38, bf16[16,96,1536]{2,1,0:T(8,128)(2,1)} %param.3, f32[16,96,1536]{2,0,1:T(8,128)} %get-tuple-element.37, f32[16,96,1536]{2,0,1:T(8,128)} %slice.154, f32[16,1,1536]{2,0,1:T(8,128)S(1)} %collective-permute-done.5, ...), kind=kLoop, calls=%fused_computation.128 | loop fusion | flops 92012544 | bytes 80412672 | tf_op jit(solution)/shard_map/add | solution.py:121
  558.6 2.6 collective-permute-start.7
  561.3 4.2 collective-permute-done.7
  565.5 71.4 %add_convert_fusion = bf16[16,96,1536]{2,0,1:T(8,128)(2,1)} fusion(f32[16,96,1536]{2,0,1:T(8,128)} %get-tuple-element.35, f32[16,96,1536]{2,0,1:T(8,128)} %get-tuple-element.36, f32[16,1,1536]{2,0,1:T(8,128)S(1)} %collective-permute-done.7, f32[16,1,1536]{2,0,1:T(8,128)S(1)} %collective-permute-done.6, bf16[16,96,1536]{2,1,0:T(8,128)(2,1)} %param.3, ...), kind=kLoop, calls=%fused_computation.98 | loop fusion | flops 89653248 | bytes 66256896 | tf_op jit(solution)/shard_map/convert_element_type | solution.py:123
  636.8 7.1 %copy.15 = bf16[16,96,1536]{2,1,0:T(8,128)(2,1)} copy(bf16[16,96,1536]{2,0,1:T(8,128)(2,1)} %add_convert_fusion) | data formatting | bytes 9437184 | tf_op jit(solution)/shard_map/convert_element_type | solution.py:123
  (24 shorter events, 16.5 us)
Async XLA Ops:
  230.2 110.5 %all-to-all-start = ((bf16[16,2,73728]{2,1,0:T(2,128)(2,1)}), bf16[16,2,73728]{2,1,0:T(2,128)(2,1)}, u32[]{:S(2)}, u32[]{:S(2)}) async-start(bf16[16,2,73728]{2,1,0:T(2,128)(2,1)} %reshape.15), calls=%async_computation | async-start | bytes 9437184 | tf_op jit(solution)/shard_map/all_to_all | solution.py:101
  395.2 12.0 %collective-permute-start = (bf16[16,1,1536]{2,0,1:T(8,128)(2,1)S(1)}, bf16[16,1,1536]{2,0,1:T(8,128)(2,1)S(1)}, u32[]{:S(2)}, u32[]{:S(2)}) collective-permute-start(bf16[16,1,1536]{2,0,1:T(8,128)(2,1)S(1)} %get-tuple-element.45), channel_id=1, source_target_pairs={{0,1},{1,2},{2,3},{3,4},{4,5},{5,6},{6,7},{7,8},{8,9},{9,10},{10,1... | collective-permute-start | bytes 147464 | tf_op jit(solution)/shard_map/ppermute | solution.py:17
  397.1 10.0 %collective-permute-start.1 = (bf16[16,1,1536]{2,0,1:T(8,128)(2,1)S(1)}, bf16[16,1,1536]{2,0,1:T(8,128)(2,1)S(1)}, u32[]{:S(2)}, u32[]{:S(2)}) collective-permute-start(bf16[16,1,1536]{2,0,1:T(8,128)(2,1)S(1)} %get-tuple-element.46), channel_id=1, source_target_pairs={{1,0},{2,1},{3,2},{4,3},{5,4},{6,5},{7,6},{8,7},{9,8},{10,9},{11,1... | collective-permute-start | bytes 147464 | tf_op jit(solution)/shard_map/ppermute | solution.py:20
  402.6 12.1 %collective-permute-start.2 = (f32[16,1,1536]{2,0,1:T(8,128)S(1)}, f32[16,1,1536]{2,0,1:T(8,128)S(1)}, u32[]{:S(2)}, u32[]{:S(2)}) collective-permute-start(f32[16,1,1536]{2,0,1:T(8,128)S(1)} %get-tuple-element.43), channel_id=1, source_target_pairs={{1,0},{2,1},{3,2},{4,3},{5,4},{6,5},{7,6},{8,7},{9,8},{10,9},{11,1... | collective-permute-start | bytes 294920 | tf_op jit(solution)/shard_map/ppermute | solution.py:20
  404.5 10.2 %collective-permute-start.3 = (f32[16,1,1536]{2,0,1:T(8,128)S(1)}, f32[16,1,1536]{2,0,1:T(8,128)S(1)}, u32[]{:S(2)}, u32[]{:S(2)}) collective-permute-start(f32[16,1,1536]{2,0,1:T(8,128)S(1)} %get-tuple-element.44), channel_id=1, source_target_pairs={{0,1},{1,2},{2,3},{3,4},{4,5},{5,6},{6,7},{7,8},{8,9},{9,10},{10,1... | collective-permute-start | bytes 294920 | tf_op jit(solution)/shard_map/ppermute | solution.py:17
  407.9 6.8 %copy-start = (f32[16,98,1536]{2,0,1:T(8,128)}, f32[16,98,1536]{2,0,1:T(8,128)S(1)}, u32[]{:S(2)}) copy-start(f32[16,98,1536]{2,0,1:T(8,128)S(1)} %maximum_convert_fusion) | copy-start | bytes 28901380
  475.0 6.3 collective-permute-start.4
  479.0 6.8 %collective-permute-start.5 = (f32[16,1,1536]{2,0,1:T(8,128)S(1)}, f32[16,1,1536]{2,0,1:T(8,128)S(1)}, u32[]{:S(2)}, u32[]{:S(2)}) collective-permute-start(f32[16,1,1536]{2,0,1:T(8,128)S(1)} %get-tuple-element.42), channel_id=1, source_target_pairs={{0,1},{1,2},{2,3},{3,4},{4,5},{5,6},{6,7},{7,8},{8,9},{9,10},{10,1... | collective-permute-start | bytes 294920 | tf_op jit(solution)/shard_map/ppermute | solution.py:17
  556.7 4.6 collective-permute-start.6
  558.6 6.8 %collective-permute-start.7 = (f32[16,1,1536]{2,0,1:T(8,128)S(1)}, f32[16,1,1536]{2,0,1:T(8,128)S(1)}, u32[]{:S(2)}, u32[]{:S(2)}) collective-permute-start(f32[16,1,1536]{2,0,1:T(8,128)S(1)} %get-tuple-element.40), channel_id=1, source_target_pairs={{0,1},{1,2},{2,3},{3,4},{4,5},{5,6},{6,7},{7,8},{8,9},{9,10},{10,1... | collective-permute-start | bytes 294920 | tf_op jit(solution)/shard_map/ppermute | solution.py:17
where the time goes:
time: 651 us; the launch traced here: 644 us
  other arithmetic  326 us (50%)
  local copies, waits for them, and re-layouts  131 us (20%)
  waiting for transfers between devices  103 us (16%)
  matrix products  55.3 us (8%)
  starting transfers between devices  28.2 us (4%)
    add x2, other arithmetic, body(): press = press + step  129 us
    all_to_all x1, waiting for transfers between devices, body(): lax.all_to_all(planes, 'wide', split_axis=1, concat_axis=0, tiled=True)  94.1 us
    convert_element_type x1, other arithmetic, body(): return press.astype(jnp.bfloat16)  71.4 us
    broadcast_in_dim x1, local copies, waits for them, and re-layouts, body(): planes = lax.map(both_axes, own_modes)  52.2 us
    dot_general x1, other arithmetic, rows_for(): jnp.dot(basis_x, coeff, preferred_element_type=jnp.float32)  45.8 us
    dot_general x1, matrix products, rows_for(): jnp.dot(basis_x, coeff, preferred_element_type=jnp.float32)  42.3 us
    dot_general x1, other arithmetic, contract_last(): lax.dot_general(left, table, (((left.ndim - 1,), (1,)), ((), ())), prefer...  36.9 us
    unnamed x1, other arithmetic  31.9 us
  transfers between devices with their start and end apart: 9, of which 4 were waited for; matrix products, arithmetic and copies ran while one was open for 3% of the time, Pallas kernels for 0%

commit v1 on v0

--- a/solution.py
+++ b/solution.py
@@ -98,7 +98,10 @@
         return contract_last(rows_for(mode_z), basis_y).astype(jnp.bfloat16)
 
     planes = lax.map(both_axes, own_modes)
-    block = lax.all_to_all(planes, "wide", split_axis=1, concat_axis=0, tiled=True)
+    block = jnp.concatenate(
+        lax.all_to_all(jnp.stack(jnp.split(planes, lax.axis_size("wide"), axis=1)), "wide", 0, 0),
+        axis=0,
+    )
     count_z, count_x, count_y = block.shape
     field = jnp.dot(
         basis_z, block.reshape(count_z, count_x * count_y), preferred_element_type=jnp.float32

time: 651 us -> 520 us (0.80)
  local copies, waits for them, and re-layouts: 131 us -> 28.2 us
  other arithmetic: 326 us -> 294 us
    broadcast_in_dim x1 -> x0, local copies, waits for them, and re-layouts: 52.2 us -> none  [body(): planes = lax.map(both_axes, own_modes)]
    unnamed x1 -> x0, other arithmetic: 31.9 us -> none
    all_to_all x1 -> x0, local copies, waits for them, and re-layouts: 31.3 us -> none  [body(): lax.all_to_all(planes, 'wide', split_axis=1, concat_axis=0, tiled=True)]
    unnamed x5 -> x17, local copies, waits for them, and re-layouts: 26.9 us -> 12.5 us
where the time goes in v1:
time: 520 us; the launch traced here: 513 us
  other arithmetic  294 us (57%)
  waiting for transfers between devices  103 us (20%)
  matrix products  58.5 us (11%)
  local copies, waits for them, and re-layouts  28.2 us (5%)
  starting transfers between devices  28.2 us (5%)
    add x2, other arithmetic, body(): press = press + step  130 us
    all_to_all x1, waiting for transfers between devices, body(): lax.all_to_all(jnp.stack(jnp.split(planes, lax.axis_size('wide'), axis=1)...  94.1 us
    convert_element_type x1, other arithmetic, body(): return press.astype(jnp.bfloat16)  71.3 us
    dot_general x1, other arithmetic, rows_for(): jnp.dot(basis_x, coeff, preferred_element_type=jnp.float32)  45.8 us
    dot_general x1, matrix products, rows_for(): jnp.dot(basis_x, coeff, preferred_element_type=jnp.float32)  42.3 us
    dot_general x1, other arithmetic, contract_last(): lax.dot_general(left, table, (((left.ndim - 1,), (1,)), ((), ())), prefer...  36.9 us
    unnamed x17, local copies, waits for them, and re-layouts  12.5 us
    ppermute x4, starting transfers between devices, with_halo(): lax.ppermute(lax.slice_in_dim(block, 0, width, axis=dim), axis, backward)  12.4 us
  transfers between devices with their start and end apart: 9, of which 4 were waited for; matrix products, arithmetic and copies ran while one was open for 3% of the time, Pallas kernels for 0%

profile of v1, /device:TPU:18, one launch (start us, length us, event | category | flops | bytes accessed | tf_op | source)
XLA Modules:
  0.0 513.5 jit_solution(8739326212134612380)
XLA Ops:
  0.7 36.9 %fusion.161 = bf16[1536,1536]{1,0:T(8,128)(2,1)S(1)} fusion(s32[1536]{0:T(1024)S(1)} %get-tuple-element.48, f32[1536]{0:T(1024)S(1)} %get-tuple-element.50), kind=kLoop, calls=%fused_computation.60.clone.clone.1 | loop fusion | flops 25952256 | bytes 4730880 | tf_op jit(solution)/shard_map/while/body/eval_jaxpr/dot_general | solution.py:60
  37.6 45.8 %multiply_convert_fusion.5 = bf16[1536,1536]{1,0:T(8,128)(2,1)S(1)} fusion(s32[]{:T(128)S(6)} %xor.65, s32[1536]{0:T(1024)S(1)} %get-tuple-element.47, f32[]{:T(128)S(6)} %mul.293, f32[1536]{0:T(1024)S(1)} %get-tuple-element.49, f32[1536]{0:T(1024)S(1)} %broadcast_add_fusion), kind=kLoop, calls=%fused_computation.101.clone.clone.2 | loop fusion | flops 103809024 | bytes 4737032 | tf_op jit(solution)/shard_map/while/body/eval_jaxpr/dot_general | solution.py:95
  83.4 42.3 %convolution_convert_fusion.1 = bf16[1536,1536]{1,0:T(8,128)(2,1)S(1)} fusion(s32[1536]{0:T(1024)S(1)} %get-tuple-element.48, f32[1536]{0:T(1024)S(1)} %get-tuple-element.50, bf16[1536,1536]{1,0:T(8,128)(2,1)S(1)} %multiply_convert_fusion.5), kind=kOutput, calls=%fused_computation.107 | convolution fusion | flops 7276068864 | bytes 9449472 | tf_op jit(solution)/shard_map/while/body/eval_jaxpr/dot_general | solution.py:95
  125.7 7.8 %fusion.71 = bf16[1,1536,1536]{2,1,0:T(8,128)(2,1)S(1)} fusion(bf16[1536,1536]{1,0:T(8,128)(2,1)S(1)} %convolution_convert_fusion.1, bf16[1536,1536]{1,0:T(8,128)(2,1)S(1)} %fusion.161), kind=kOutput, calls=%fused_computation.108 | convolution fusion | flops 7250116608 | bytes 14155776 | tf_op jit(solution)/shard_map/while/body/eval_jaxpr/dot_general | solution.py:60
  145.2 6.5 %all-to-all-start = ((bf16[16,1,96,1536]{3,2,1,0:T(8,128)(2,1)}), bf16[16,1,96,1536]{3,2,1,0:T(8,128)(2,1)}, u32[]{:S(2)}, u32[]{:S(2)}) async-start(bf16[16,1,96,1536]{3,2,1,0:T(8,128)(2,1)} %fusion.93), calls=%async_computation | async-start | bytes 9437184 | tf_op jit(solution)/shard_map/all_to_all | solution.py:102
  151.8 9.6 %convert_multiply_fusion.1 = f32[16,96,1536]{2,0,1:T(8,128)} fusion(bf16[16,96,1536]{2,1,0:T(8,128)(2,1)} %param.3), kind=kLoop, calls=%fused_computation.4 | loop fusion | flops 4718592 | bytes 14155776 | tf_op jit(solution)/shard_map/div | solution.py:116
  161.4 94.1 %all-to-all-done = bf16[16,1,96,1536]{3,2,1,0:T(8,128)(2,1)} async-done(((bf16[16,1,96,1536]{3,2,1,0:T(8,128)(2,1)}), bf16[16,1,96,1536]{3,2,1,0:T(8,128)(2,1)}, u32[]{:S(2)}, u32[]{:S(2)}) %all-to-all-start) | async-done | bytes 4718624 | tf_op jit(solution)/shard_map/all_to_all | solution.py:102
  255.5 8.4 %exponential_convert_fusion = bf16[16,96,1536]{2,0,1:T(8,128)(2,1)S(1)} fusion(s32[16]{0:T(128)S(1)} %multiply_add_fusion.2, f32[16]{0:T(128)S(1)} %compare_select_fusion, bf16[2,8,96,1536]{3,2,1,0:T(8,128)(2,1)} %bitcast.23), kind=kOutput, calls=%fused_computation.100 | convolution fusion | flops 82579456 | bytes 9437312 | tf_op jit(solution)/shard_map/dot_general | solution.py:106
  264.0 1.9 collective-permute-start
  265.9 4.5 collective-permute-start.1
  271.4 1.9 collective-permute-start.2
  273.4 2.8 collective-permute-start.3
  277.0 4.9 slice.154
  281.9 1.5 copy-done
  283.4 59.9 %fusion = (f32[16,96,1536]{2,0,1:T(8,128)}, f32[16,96,1536]{2,0,1:T(8,128)}) fusion(bf16[16,96,1536]{2,1,0:T(8,128)(2,1)} %param.3, f32[16,96,1536]{2,0,1:T(8,128)} %slice.154, f32[16,96,1536]{2,0,1:T(8,128)} %convert_multiply_fusion.1, f32[16,1,1536]{2,0,1:T(8,128)S(1)} %collective-permute-done.3, f32[16,98,1536]{2,0,1:T(8,128)} %copy-done, ...), kind=kLoop, calls=%fused_computation.14 | loop fusion | flops 89653248 | bytes 70975488 | tf_op jit(solution)/shard_map/add | solution.py:124
  344.3 4.1 collective-permute-start.4
  348.4 1.9 collective-permute-start.5
  350.6 4.6 collective-permute-done.5
  355.2 69.9 %fusion.92 = (f32[16,96,1536]{2,0,1:T(8,128)}, f32[16,96,1536]{2,0,1:T(8,128)}) fusion(f32[16,96,1536]{2,0,1:T(8,128)} %get-tuple-element.38, bf16[16,96,1536]{2,1,0:T(8,128)(2,1)} %param.3, f32[16,96,1536]{2,0,1:T(8,128)} %get-tuple-element.37, f32[16,96,1536]{2,0,1:T(8,128)} %slice.154, f32[16,1,1536]{2,0,1:T(8,128)S(1)} %collective-permute-done.5, ...), kind=kLoop, calls=%fused_computation.128 | loop fusion | flops 92012544 | bytes 80412672 | tf_op jit(solution)/shard_map/add | solution.py:124
  426.1 1.9 collective-permute-start.6
  428.1 2.6 collective-permute-start.7
  430.7 4.2 collective-permute-done.7
  434.9 71.3 %add_convert_fusion = bf16[16,96,1536]{2,0,1:T(8,128)(2,1)} fusion(f32[16,96,1536]{2,0,1:T(8,128)} %get-tuple-element.35, f32[16,96,1536]{2,0,1:T(8,128)} %get-tuple-element.36, f32[16,1,1536]{2,0,1:T(8,128)S(1)} %collective-permute-done.7, f32[16,1,1536]{2,0,1:T(8,128)S(1)} %collective-permute-done.6, bf16[16,96,1536]{2,1,0:T(8,128)(2,1)} %param.3, ...), kind=kLoop, calls=%fused_computation.98 | loop fusion | flops 89653248 | bytes 66256896 | tf_op jit(solution)/shard_map/convert_element_type | solution.py:126
  506.2 7.1 %copy.7 = bf16[16,96,1536]{2,1,0:T(8,128)(2,1)} copy(bf16[16,96,1536]{2,0,1:T(8,128)(2,1)} %add_convert_fusion) | data formatting | bytes 9437184 | tf_op jit(solution)/shard_map/convert_element_type | solution.py:126
  (33 shorter events, 15.7 us)
Async XLA Ops:
  145.2 110.3 %all-to-all-start = ((bf16[16,1,96,1536]{3,2,1,0:T(8,128)(2,1)}), bf16[16,1,96,1536]{3,2,1,0:T(8,128)(2,1)}, u32[]{:S(2)}, u32[]{:S(2)}) async-start(bf16[16,1,96,1536]{3,2,1,0:T(8,128)(2,1)} %fusion.93), calls=%async_computation | async-start | bytes 9437184 | tf_op jit(solution)/shard_map/all_to_all | solution.py:102
  264.0 12.2 %collective-permute-start = (bf16[16,1,1536]{2,0,1:T(8,128)(2,1)S(1)}, bf16[16,1,1536]{2,0,1:T(8,128)(2,1)S(1)}, u32[]{:S(2)}, u32[]{:S(2)}) collective-permute-start(bf16[16,1,1536]{2,0,1:T(8,128)(2,1)S(1)} %get-tuple-element.45), channel_id=1, source_target_pairs={{0,1},{1,2},{2,3},{3,4},{4,5},{5,6},{6,7},{7,8},{8,9},{9,10},{10,1... | collective-permute-start | bytes 147464 | tf_op jit(solution)/shard_map/ppermute | solution.py:17
  265.9 10.3 %collective-permute-start.1 = (bf16[16,1,1536]{2,0,1:T(8,128)(2,1)S(1)}, bf16[16,1,1536]{2,0,1:T(8,128)(2,1)S(1)}, u32[]{:S(2)}, u32[]{:S(2)}) collective-permute-start(bf16[16,1,1536]{2,0,1:T(8,128)(2,1)S(1)} %get-tuple-element.46), channel_id=1, source_target_pairs={{1,0},{2,1},{3,2},{4,3},{5,4},{6,5},{7,6},{8,7},{9,8},{10,9},{11,1... | collective-permute-start | bytes 147464 | tf_op jit(solution)/shard_map/ppermute | solution.py:20
  271.4 12.0 %collective-permute-start.2 = (f32[16,1,1536]{2,0,1:T(8,128)S(1)}, f32[16,1,1536]{2,0,1:T(8,128)S(1)}, u32[]{:S(2)}, u32[]{:S(2)}) collective-permute-start(f32[16,1,1536]{2,0,1:T(8,128)S(1)} %get-tuple-element.43), channel_id=1, source_target_pairs={{1,0},{2,1},{3,2},{4,3},{5,4},{6,5},{7,6},{8,7},{9,8},{10,9},{11,1... | collective-permute-start | bytes 294920 | tf_op jit(solution)/shard_map/ppermute | solution.py:20
  273.4 10.1 %collective-permute-start.3 = (f32[16,1,1536]{2,0,1:T(8,128)S(1)}, f32[16,1,1536]{2,0,1:T(8,128)S(1)}, u32[]{:S(2)}, u32[]{:S(2)}) collective-permute-start(f32[16,1,1536]{2,0,1:T(8,128)S(1)} %get-tuple-element.44), channel_id=1, source_target_pairs={{0,1},{1,2},{2,3},{3,4},{4,5},{5,6},{6,7},{7,8},{8,9},{9,10},{10,1... | collective-permute-start | bytes 294920 | tf_op jit(solution)/shard_map/ppermute | solution.py:17
  277.0 6.5 %copy-start = (f32[16,98,1536]{2,0,1:T(8,128)}, f32[16,98,1536]{2,0,1:T(8,128)S(1)}, u32[]{:S(2)}) copy-start(f32[16,98,1536]{2,0,1:T(8,128)S(1)} %maximum_convert_fusion) | copy-start | bytes 28901380
  344.3 6.3 %collective-permute-start.4 = (f32[16,1,1536]{2,0,1:T(8,128)S(1)}, f32[16,1,1536]{2,0,1:T(8,128)S(1)}, u32[]{:S(2)}, u32[]{:S(2)}) collective-permute-start(f32[16,1,1536]{2,0,1:T(8,128)S(1)} %get-tuple-element.41), channel_id=1, source_target_pairs={{1,0},{2,1},{3,2},{4,3},{5,4},{6,5},{7,6},{8,7},{9,8},{10,9},{11,1... | collective-permute-start | bytes 294920 | tf_op jit(solution)/shard_map/ppermute | solution.py:20
  348.4 6.8 %collective-permute-start.5 = (f32[16,1,1536]{2,0,1:T(8,128)S(1)}, f32[16,1,1536]{2,0,1:T(8,128)S(1)}, u32[]{:S(2)}, u32[]{:S(2)}) collective-permute-start(f32[16,1,1536]{2,0,1:T(8,128)S(1)} %get-tuple-element.42), channel_id=1, source_target_pairs={{0,1},{1,2},{2,3},{3,4},{4,5},{5,6},{6,7},{7,8},{8,9},{9,10},{10,1... | collective-permute-start | bytes 294920 | tf_op jit(solution)/shard_map/ppermute | solution.py:17
  426.1 4.5 collective-permute-start.6
  428.1 6.8 %collective-permute-start.7 = (f32[16,1,1536]{2,0,1:T(8,128)S(1)}, f32[16,1,1536]{2,0,1:T(8,128)S(1)}, u32[]{:S(2)}, u32[]{:S(2)}) collective-permute-start(f32[16,1,1536]{2,0,1:T(8,128)S(1)} %get-tuple-element.40), channel_id=1, source_target_pairs={{0,1},{1,2},{2,3},{3,4},{4,5},{5,6},{6,7},{7,8},{8,9},{9,10},{10,1... | collective-permute-start | bytes 294920 | tf_op jit(solution)/shard_map/ppermute | solution.py:17
